TPU v7x, 32 devices: a whole 2x2x4 slice. The times are simulated.
32 devices in a mesh: seq: 16 (over z, x, core), tp: 2 (over y).
Axes of the slice: x: 2, y: 2, z: 4, core: 2. Of those that a mesh axis runs over, the one named last changes fastest.
Arguments:
- normed_input: bfloat16 [2048, 4096], P(('seq', 'tp')), may hold values from -6 to 6
- output_gradient: bfloat16 [2048, 14336], P('seq', 'tp'), may hold values from -0.75 to 0.75
- adapter_down: bfloat16 [64, 16, 4096], P('seq', None, 'tp'), may hold values from -0.09375 to 0.09375
- adapter_up: bfloat16 [64, 16, 14336], P('seq', None, 'tp'), may hold values from -1.5 to 1.5
- adapter_of_block: int32 [16], P('seq'), may hold values from 0 to 63
- live_per_block: int32 [16], P('seq'), may hold values from 32 to 128, as said below
- adapter_home_row: int32 [64], replicated, may hold values from 0 to 63, each once
Outputs:
- adapter_output: bfloat16 [2048, 14336], P('seq', 'tp')
- input_gradient: bfloat16 [2048, 4096], P(('seq', 'tp'))
- down_gradient: float32 [64, 16, 4096], P('seq', None, 'tp')
- up_gradient: float32 [64, 16, 14336], P('seq', None, 'tp')
Inputs may be any that keep to these rules, and one draw needn't show every extreme that they name: `live_per_block`: every eighth block, counting from block 0, is full. `adapter_home_row`: each row appears once.
All inputs are finite; a program needn't handle non-finite values.
Results may differ from a plain program's by a relative error of at most 0.0051.
Values may be sent and summed in bfloat16 or wider, within the bound.
A program may use at most 128 MiB of HBM per device.

v0:
```python
import jax
import jax.numpy as jnp
from jax import lax
from jax.sharding import PartitionSpec as P

adapter_scale = 2.0


def per_device(
    normed_input,
    output_gradient,
    adapter_down,
    adapter_up,
    adapter_of_block,
    live_per_block,
    adapter_home_row,
):
    seq_count = lax.axis_size("seq")
    total_blocks = adapter_of_block.shape[0]
    token_rows = output_gradient.shape[0]
    block_length = token_rows // total_blocks
    adapters = adapter_home_row.shape[0]
    rank_projected = adapter_down.shape[1]
    width_slice = adapter_down.shape[2]
    hidden_slice = adapter_up.shape[2]
    all_a, all_b = (
        lax.all_gather(adapter_down, "seq", axis=0, tiled=True),
        lax.all_gather(adapter_up, "seq", axis=0, tiled=True),
    )
    chosen = (adapter_of_block[:, None] == jnp.arange(adapters, dtype=jnp.int32)[None, :]).astype(
        jnp.float32
    )
    chosen_low = chosen.astype(jnp.bfloat16)
    pick_a = jnp.einsum(
        "ba,ard->brd", chosen_low, all_a, preferred_element_type=jnp.float32
    ).astype(jnp.bfloat16)
    pick_b = jnp.einsum(
        "ba,arf->brf", chosen_low, all_b, preferred_element_type=jnp.float32
    ).astype(jnp.bfloat16)
    token_live_mask = (
        jnp.arange(block_length, dtype=jnp.int32)[None, :] < live_per_block[:, None]
    ).astype(jnp.float32)[:, :, None]
    g_blocks = output_gradient.reshape(total_blocks, block_length, hidden_slice)
    back_part = jnp.einsum("btf,brf->btr", g_blocks, pick_b, preferred_element_type=jnp.float32)
    back_part = back_part.reshape(total_blocks, block_length * rank_projected)
    x_tensor = lax.all_to_all(normed_input, "tp", split_axis=1, concat_axis=0, tiled=True)
    x_blocks = x_tensor.reshape(total_blocks, block_length, width_slice)
    down_part = jnp.einsum("btd,brd->btr", x_blocks, pick_a, preferred_element_type=jnp.float32)
    down_part = down_part.reshape(total_blocks, block_length * rank_projected)
    down_sum, backward_total = lax.psum((down_part, back_part), "tp")
    down_reduced = (
        down_sum.reshape(total_blocks, block_length, rank_projected) * token_live_mask
    ).astype(jnp.bfloat16)
    backward_reduced = (
        adapter_scale
        * backward_total.reshape(total_blocks, block_length, rank_projected)
        * token_live_mask
    ).astype(jnp.bfloat16)
    grad_tensor = jnp.einsum(
        "btr,brd->btd", backward_reduced, pick_a, preferred_element_type=jnp.float32
    )
    grad_tensor = grad_tensor.astype(jnp.bfloat16).reshape(token_rows, width_slice)
    input_gradient = lax.all_to_all(grad_tensor, "tp", split_axis=0, concat_axis=1, tiled=True)
    grad_a_blocks = jnp.einsum(
        "btr,btd->brd", backward_reduced, x_blocks, preferred_element_type=jnp.float32
    )
    adapter_output = adapter_scale * jnp.einsum(
        "btr,brf->btf", down_reduced, pick_b, preferred_element_type=jnp.float32
    )
    adapter_output = adapter_output.astype(jnp.bfloat16).reshape(token_rows, hidden_slice)
    up_gradient_blocks = adapter_scale * jnp.einsum(
        "btr,btf->brf", down_reduced, g_blocks, preferred_element_type=jnp.float32
    )
    block_row = jnp.dot(
        chosen, adapter_home_row.astype(jnp.float32), precision=lax.Precision.HIGHEST
    )
    slots_each = adapters // seq_count
    my_rows = (lax.axis_index("seq") * slots_each + jnp.arange(slots_each, dtype=jnp.int32)).astype(
        jnp.float32
    )
    piece_a = lax.all_gather(grad_a_blocks, "seq", axis=0, tiled=True)
    piece_b = lax.all_gather(up_gradient_blocks, "seq", axis=0, tiled=True)
    piece_rows = lax.all_gather(block_row, "seq", axis=0, tiled=True)
    match = (piece_rows[:, None] == my_rows[None, :]).astype(jnp.float32)
    following_down = jnp.einsum("ns,nrd->srd", match, piece_a, precision=lax.Precision.HIGHEST)
    following_up = jnp.einsum("ns,nrf->srf", match, piece_b, precision=lax.Precision.HIGHEST)
    return (adapter_output, input_gradient, following_down, following_up)


def solution(mesh):
    placed = (
        P(("seq", "tp"), None),
        P("seq", "tp"),
        P("seq", None, "tp"),
        P("seq", None, "tp"),
        P("seq"),
        P("seq"),
        P(),
    )
    return jax.shard_map(
        per_device,
        mesh=mesh,
        in_specs=placed,
        out_specs=(
            P("seq", "tp"),
            P(("seq", "tp"), None),
            P("seq", None, "tp"),
            P("seq", None, "tp"),
        ),
        check_vma=False,
    )
```

profile of v0, /device:TPU:0, one launch (start us, length us, event | category | flops | bytes accessed | tf_op | source)
XLA Modules:
  0.0 334.9 jit_solution(5447570768813441117)
XLA Ops:
  7.2 0.7 all-gather.7.cloned.1.call-update
  8.0 0.7 all-gather.9.cloned.1.call-update
  8.7 1.9 copy.62
  10.5 4.3 %all-to-all-start = ((bf16[64,2,2048]{2,0,1:T(8,128)(2,1)}), bf16[64,2,2048]{2,0,1:T(8,128)(2,1)S(1)}, u32[]{:S(2)}, u32[]{:S(2)}) async-start(bf16[64,2,2048]{2,0,1:T(8,128)(2,1)} %bitcast.50), calls=%async_computation | async-start | bytes 1048576 | tf_op jit(solution)/shard_map/all_to_all | solution.py:46
  16.5 46.8 %all-gather.7.cloned.1.call-done = bf16[64,16,2048]{2,1,0:T(8,128)(2,1)} async-done(((bf16[4,16,2048]{2,1,0:T(8,128)(2,1)}), bf16[64,16,2048]{2,1,0:T(8,128)(2,1)}) %all-gather.7.cloned.1.call-update) | async-done | bytes 4194320 | tf_op jit(solution)/shard_map/all_gather | solution.py:27
  63.3 6.7 %fusion.5 = bf16[1,16,2048]{2,0,1:T(2,128)(2,1)S(1)} fusion(bf16[64,16,2048]{2,1,0:T(8,128)(2,1)} %all-gather.7.cloned.1.call-done, s32[]{:T(128)} %bitcast.51), kind=kOutput, calls=%fused_computation.7 | convolution fusion | flops 4194496 | bytes 4259844 | tf_op jit(solution)/shard_map/ba,ard->brd/dot_general | solution.py:34
  70.4 107.1 %all-gather.9.cloned.1.call-done = bf16[64,16,7168]{2,1,0:T(8,128)(2,1)} async-done(((bf16[4,16,7168]{2,1,0:T(8,128)(2,1)}), bf16[64,16,7168]{2,1,0:T(8,128)(2,1)}) %all-gather.9.cloned.1.call-update) | async-done | bytes 14680080 | tf_op jit(solution)/shard_map/all_gather | solution.py:28
  177.5 20.9 %fusion = bf16[1,16,7168]{2,0,1:T(2,128)(2,1)S(1)} fusion(bf16[64,16,7168]{2,1,0:T(8,128)(2,1)} %all-gather.9.cloned.1.call-done, s32[]{:T(128)} %bitcast.52), kind=kOutput, calls=%fused_computation | convolution fusion | flops 14680256 | bytes 14909444 | tf_op jit(solution)/shard_map/ba,arf->brf/dot_general | solution.py:37
  199.2 8.1 %all-reduce.1 = (f32[1,2048]{1,0:T(1,128)S(1)}, f32[1,2048]{1,0:T(1,128)S(1)}) all-reduce(f32[1,2048]{1,0:T(1,128)S(1)} %reshape.142, f32[1,2048]{1,0:T(1,128)S(1)} %reshape.143), channel_id=1, replica_groups=mesh['seq'=16,'tp'=2] {'tp'}, use_global_device_ids=true, to_apply=%region_0.0 | all-reduce | flops 4096 | bytes 32768 | tf_op jit(solution)/shard_map/psum | solution.py:50
  207.4 0.9 fusion.24
  208.4 1.2 convolution_multiply_fusion.1
  210.2 0.6 fusion.19
  210.8 1.4 dynamic-update-slice
  212.2 30.0 %all-reduce = f32[16]{0:T(128)S(1)} all-reduce(f32[16]{0:T(128)S(1)} %dynamic-update-slice), channel_id=1, replica_groups=mesh['seq'=16,'tp'=2] {'seq'}, use_global_device_ids=true, to_apply=%add | all-reduce | flops 16 | bytes 128
  242.2 1.1 convolution_convert_fusion
  243.3 3.7 %all-to-all-start.1 = ((bf16[2,64,2048]{2,1,0:T(8,128)(2,1)}), bf16[2,64,2048]{2,1,0:T(8,128)(2,1)S(1)}, u32[]{:S(2)}, u32[]{:S(2)}) async-start(bf16[2,64,2048]{2,1,0:T(8,128)(2,1)} %bitcast.10), calls=%async_computation.1 | async-start | bytes 1048576 | tf_op jit(solution)/shard_map/all_to_all | solution.py:63
  247.0 1.8 fusion.2
  248.9 6.0 %all-to-all-done.1 = bf16[2,64,2048]{2,1,0:T(8,128)(2,1)S(1)} async-done(((bf16[2,64,2048]{2,1,0:T(8,128)(2,1)}), bf16[2,64,2048]{2,1,0:T(8,128)(2,1)S(1)}, u32[]{:S(2)}, u32[]{:S(2)}) %all-to-all-start.1) | async-done | bytes 524320 | tf_op jit(solution)/shard_map/all_to_all | solution.py:63
  254.9 0.8 copy.46
  255.7 3.6 %fusion.7 = f32[4,16,2048]{2,0,1:T(4,128)S(1)} fusion(f32[16,16,2048]{2,1,0:T(8,128)} %bitcast.59, f32[16]{0:T(128)S(1)} %all-reduce, f32[4]{0:T(128)S(1)} %add_convert_fusion), kind=kOutput, calls=%fused_computation.10 | convolution fusion | flops 25165888 | bytes 2621520 | tf_op jit(solution)/shard_map/ns,nrd->srd/dot_general | solution.py:85
  259.3 1.1 copy.37
  260.4 56.1 %all-gather.13.cloned.1.call-done = f32[256,7168]{1,0:T(8,128)} async-done(((f32[16,7168]{1,0:T(8,128)}), f32[256,7168]{1,0:T(8,128)}) %all-gather.13.cloned.1.call-update) | async-done | bytes 7340048 | tf_op jit(solution)/shard_map/all_gather | solution.py:82
  316.5 9.5 %fusion.3 = f32[4,16,7168]{2,0,1:T(4,128)S(1)} fusion(f32[16,16,7168]{2,1,0:T(8,128)} %bitcast.56, f32[16]{0:T(128)S(1)} %all-reduce, f32[4]{0:T(128)S(1)} %add_convert_fusion), kind=kOutput, calls=%fused_computation.5 | convolution fusion | flops 88080448 | bytes 9175120 | tf_op jit(solution)/shard_map/ns,nrf->srf/dot_general | solution.py:86
  326.1 2.3 copy.38
  (32 shorter events, 2.6 us)
Async XLA Ops:
  7.2 191.2 %copy-start = (bf16[128,7168]{1,0:T(8,128)(2,1)S(1)}, bf16[128,7168]{1,0:T(8,128)(2,1)}, u32[]{:S(2)}) copy-start(bf16[128,7168]{1,0:T(8,128)(2,1)} %param.8) | copy-start | bytes 5505028
  7.2 56.1 %all-gather.7.cloned.1.call-start = ((), (), s32[]{:S(2)}) async-start(), calls=%async_computation.2 | async-start | bytes 4456448 | tf_op jit(solution)/shard_map/all_gather | solution.py:27
  7.9 169.6 %all-gather.9.cloned.1.call-start = ((), (), s32[]{:S(2)}) async-start(), calls=%async_computation.3 | async-start | bytes 15597568 | tf_op jit(solution)/shard_map/all_gather | solution.py:28
  10.5 59.4 %all-to-all-start = ((bf16[64,2,2048]{2,0,1:T(8,128)(2,1)}), bf16[64,2,2048]{2,0,1:T(8,128)(2,1)S(1)}, u32[]{:S(2)}, u32[]{:S(2)}) async-start(bf16[64,2,2048]{2,0,1:T(8,128)(2,1)} %bitcast.50), calls=%async_computation | async-start | bytes 1048576 | tf_op jit(solution)/shard_map/all_to_all | solution.py:46
  14.8 240.9 %all-gather.11.cloned.1.call-start = ((), (), s32[]{:S(2)}) async-start(), calls=%async_computation.4 | async-start | bytes 2228224 | tf_op jit(solution)/shard_map/all_gather | solution.py:81
  198.4 11.3 %copy-start.2 = (u32[32]{0:T(128)S(1)}, u32[32]{0:T(128)}, u32[]{:S(2)}) copy-start(u32[32]{0:T(128)} %constant.20) | copy-start | bytes 388
  198.4 11.9 %copy-start.1 = (s32[64]{0:T(128)S(1)}, s32[64]{0:T(128)}, u32[]{:S(2)}) copy-start(s32[64]{0:T(128)} %param.13) | copy-start | bytes 772
  208.3 108.2 %all-gather.13.cloned.1.call-start = ((), (), s32[]{:S(2)}) async-start(), calls=%async_computation.5 | async-start | bytes 7798784 | tf_op jit(solution)/shard_map/all_gather | solution.py:82
  243.3 11.6 %all-to-all-start.1 = ((bf16[2,64,2048]{2,1,0:T(8,128)(2,1)}), bf16[2,64,2048]{2,1,0:T(8,128)(2,1)S(1)}, u32[]{:S(2)}, u32[]{:S(2)}) async-start(bf16[2,64,2048]{2,1,0:T(8,128)(2,1)} %bitcast.10), calls=%async_computation.1 | async-start | bytes 1048576 | tf_op jit(solution)/shard_map/all_to_all | solution.py:63
Sparse Core Ops, SparseCore 0:
  10.1 53.0 all-gather.6
  65.6 111.8 all-gather.8
  208.4 38.7 all-gather.10
  249.9 66.5 all-gather.12
where the time goes:
time: 335 us
  waiting for transfers between devices  217 us (65%)
  matrix products  46.5 us (14%)
  blocking collectives  38 us (11%)
  between operations  15.2 us (5%)
  local copies, waits for them, and re-layouts  9.04 us (3%)
  starting transfers between devices  8.09 us (2%)
    all_gather x1, waiting for transfers between devices, per_device(): lax.all_gather(adapter_up, 'seq', axis=0, tiled=True)  107 us
    all_gather x1, waiting for transfers between devices, per_device(): piece_b = lax.all_gather(up_gradient_blocks, 'seq', axis=0, tiled=True)  56.1 us
    all_gather x1, waiting for transfers between devices, per_device(): lax.all_gather(adapter_down, 'seq', axis=0, tiled=True)  46.8 us
    unnamed x1, blocking collectives  30 us
    dot_general x1, matrix products, per_device(): jnp.einsum('ba,arf->brf', chosen_low, all_b, preferred_element_type=jnp.f...  20.9 us
    dot_general x1, matrix products, per_device(): jnp.einsum('ns,nrf->srf', match, piece_b, precision=lax.Precision.HIGHEST)  9.53 us
    psum x1, blocking collectives, per_device(): down_sum, backward_total = lax.psum((down_part, back_part), 'tp')  8.06 us
    dot_general x1, matrix products, per_device(): jnp.einsum('ba,ard->brd', chosen_low, all_a, preferred_element_type=jnp.f...  6.7 us
  transfers between devices with their start and end apart: 6, of which 4 were waited for; matrix products, arithmetic and copies ran while one was open for 6% of the time, Pallas kernels for 0%

commit v1 on v0

--- a/solution.py
+++ b/solution.py
@@ -4,6 +4,22 @@
 from jax.sharding import PartitionSpec as P
 
 adapter_scale = 2.0
+
+
+def product_in_turn(x, axis, dim, term):
+    size, index, width = (lax.axis_size(axis), lax.axis_index(axis), x.shape[dim])
+    right = [(i, (i + 1) % size) for i in range(size)]
+    backward = [(i, (i - 1) % size) for i in range(size)]
+    half = size // 2
+    from_left = from_right = x
+    total = term(x, index * width)
+    for hop in range(1, half + 1):
+        from_left = lax.ppermute(from_left, axis, right)
+        if hop < size - half:
+            from_right = lax.ppermute(from_right, axis, backward)
+            total = total + term(from_right, (index + hop) % size * width)
+        total = total + term(from_left, (index - hop) % size * width)
+    return total
 
 
 def per_device(
@@ -79,11 +95,20 @@
         jnp.float32
     )
     piece_a = lax.all_gather(grad_a_blocks, "seq", axis=0, tiled=True)
-    piece_b = lax.all_gather(up_gradient_blocks, "seq", axis=0, tiled=True)
     piece_rows = lax.all_gather(block_row, "seq", axis=0, tiled=True)
     match = (piece_rows[:, None] == my_rows[None, :]).astype(jnp.float32)
     following_down = jnp.einsum("ns,nrd->srd", match, piece_a, precision=lax.Precision.HIGHEST)
-    following_up = jnp.einsum("ns,nrf->srf", match, piece_b, precision=lax.Precision.HIGHEST)
+    following_up = product_in_turn(
+        up_gradient_blocks,
+        "seq",
+        0,
+        lambda shard, at: jnp.einsum(
+            "ns,nrf->srf",
+            lax.dynamic_slice_in_dim(match, at, shard.shape[0], axis=0),
+            shard,
+            precision=lax.Precision.HIGHEST,
+        ),
+    )
     return (adapter_output, input_gradient, following_down, following_up)
 
 

time: 335 us -> 351 us (1.048)
  starting transfers between devices: 8.09 us -> 46.3 us
  waiting for transfers between devices: 217 us -> 196 us
  matrix products: 46.5 us -> 36.1 us
  other arithmetic: 0.67 us -> 7.12 us
  blocking collectives: 38 us -> 42.9 us
    all_gather x1 -> x0, waiting for transfers between devices: 56.1 us -> none  [per_device(): piece_b = lax.all_gather(up_gradient_blocks, 'seq', axis=0, tiled=True)]
    ppermute x0 -> x15, starting transfers between devices: none -> 36.5 us  [the longest x8 21.4 us: product_in_turn(): from_left = lax.ppermute(from_left, axis, right)]
    ppermute x0 -> x15, waiting for transfers between devices: none -> 33.3 us  [the longest x8 33.2 us: product_in_turn(): from_left = lax.ppermute(from_left, axis, right)]
    dot_general x1 -> x0, matrix products: 9.53 us -> none  [per_device(): jnp.einsum('ns,nrf->srf', match, piece_b, precision=lax.Precision.HIGHEST)]
    add x0 -> x1, other arithmetic: none -> 6.34 us  [product_in_turn(): total = total + term(from_left, (index - hop) % size * width)]
    unnamed x1, blocking collectives: 30 us -> 34.9 us
  transfers between devices with their start and end apart: 6 -> 20, of which waited for: 4 -> 9; matrix products, arithmetic and copies ran while one was open for 6% -> 7% of each run, Pallas kernels for 0% -> 0%
where the time goes in v1:
time: 351 us
  waiting for transfers between devices  196 us (56%)
  starting transfers between devices  46.3 us (13%)
  blocking collectives  42.9 us (12%)
  matrix products  36.1 us (10%)
  between operations  15.4 us (4%)
  local copies, waits for them, and re-layouts  7.21 us (2%)
  other arithmetic  7.12 us (2%)
    all_gather x1, waiting for transfers between devices, per_device(): lax.all_gather(adapter_up, 'seq', axis=0, tiled=True)  107 us
    all_gather x1, waiting for transfers between devices, per_device(): lax.all_gather(adapter_down, 'seq', axis=0, tiled=True)  46.8 us
    unnamed x1, blocking collectives  34.9 us
    ppermute x8, waiting for transfers between devices, product_in_turn(): from_left = lax.ppermute(from_left, axis, right)  33.2 us
    ppermute x8, starting transfers between devices, product_in_turn(): from_left = lax.ppermute(from_left, axis, right)  21.4 us
    dot_general x1, matrix products, per_device(): jnp.einsum('ba,arf->brf', chosen_low, all_b, preferred_element_type=jnp.f...  20.9 us
    ppermute x7, starting transfers between devices, product_in_turn(): from_right = lax.ppermute(from_right, axis, backward)  15.1 us
    psum x1, blocking collectives, per_device(): down_sum, backward_total = lax.psum((down_part, back_part), 'tp')  8.06 us
  transfers between devices with their start and end apart: 20, of which 9 were waited for; matrix products, arithmetic and copies ran while one was open for 7% of the time, Pallas kernels for 0%

profile of v1, /device:TPU:0, one launch (start us, length us, event | category | flops | bytes accessed | tf_op | source)
XLA Modules:
  0.0 350.7 jit_solution(7498619708754323797)
XLA Ops:
  10.5 4.3 %all-to-all-start = ((bf16[64,2,2048]{2,0,1:T(8,128)(2,1)}), bf16[64,2,2048]{2,0,1:T(8,128)(2,1)S(1)}, u32[]{:S(2)}, u32[]{:S(2)}) async-start(bf16[64,2,2048]{2,0,1:T(8,128)(2,1)} %bitcast.95), calls=%async_computation | async-start | bytes 1048576 | tf_op jit(solution)/shard_map/all_to_all | solution.py:62
  16.5 46.8 %all-gather.5.cloned.1.call-done = bf16[64,16,2048]{2,1,0:T(8,128)(2,1)} async-done(((bf16[4,16,2048]{2,1,0:T(8,128)(2,1)}), bf16[64,16,2048]{2,1,0:T(8,128)(2,1)}) %all-gather.5.cloned.1.call-update) | async-done | bytes 4194320 | tf_op jit(solution)/shard_map/all_gather | solution.py:43
  63.3 6.7 %fusion.3 = bf16[1,16,2048]{2,0,1:T(2,128)(2,1)S(1)} fusion(bf16[64,16,2048]{2,1,0:T(8,128)(2,1)} %all-gather.5.cloned.1.call-done, s32[]{:T(128)} %bitcast.96), kind=kOutput, calls=%fused_computation.5 | convolution fusion | flops 4194496 | bytes 4259844 | tf_op jit(solution)/shard_map/ba,ard->brd/dot_general | solution.py:50
  70.4 107.1 %all-gather.7.cloned.1.call-done = bf16[64,16,7168]{2,1,0:T(8,128)(2,1)} async-done(((bf16[4,16,7168]{2,1,0:T(8,128)(2,1)}), bf16[64,16,7168]{2,1,0:T(8,128)(2,1)}) %all-gather.7.cloned.1.call-update) | async-done | bytes 14680080 | tf_op jit(solution)/shard_map/all_gather | solution.py:44
  177.5 20.9 %fusion = bf16[1,16,7168]{2,0,1:T(2,128)(2,1)S(1)} fusion(bf16[64,16,7168]{2,1,0:T(8,128)(2,1)} %all-gather.7.cloned.1.call-done, s32[]{:T(128)} %bitcast.97), kind=kOutput, calls=%fused_computation | convolution fusion | flops 14680256 | bytes 14909444 | tf_op jit(solution)/shard_map/ba,arf->brf/dot_general | solution.py:53
  199.2 8.1 %all-reduce.1 = (f32[1,2048]{1,0:T(1,128)S(1)}, f32[1,2048]{1,0:T(1,128)S(1)}) all-reduce(f32[1,2048]{1,0:T(1,128)S(1)} %reshape.269, f32[1,2048]{1,0:T(1,128)S(1)} %reshape.270), channel_id=1, replica_groups=mesh['seq'=16,'tp'=2] {'tp'}, use_global_device_ids=true, to_apply=%region_0.0 | all-reduce | flops 4096 | bytes 32768 | tf_op jit(solution)/shard_map/psum | solution.py:66
  207.8 4.4 %collective-permute-start = (f32[1,16,7168]{2,1,0:T(8,128)S(1)}, f32[1,16,7168]{2,1,0:T(8,128)}, u32[]{:S(2)}, u32[]{:S(2)}) collective-permute-start(f32[1,16,7168]{2,1,0:T(8,128)S(1)} %bitcast.106), channel_id=1, source_target_pairs={{0,30},{2,0},{4,2},{6,4},{8,6},{10,8},{12,10},{14,12},{16,14},{18,... | collective-permute-start | bytes 1376264 | tf_op jit(solution)/shard_map/ppermute | solution.py:19
  212.3 6.3 %collective-permute-done.1 = f32[1,16,7168]{2,1,0:T(8,128)S(1)} collective-permute-done((f32[1,16,7168]{2,1,0:T(8,128)S(1)}, f32[1,16,7168]{2,1,0:T(8,128)S(1)}, u32[]{:S(2)}, u32[]{:S(2)}) %collective-permute-start.1) | collective-permute-done | bytes 458784 | tf_op jit(solution)/shard_map/ppermute | solution.py:17
  219.3 3.8 %collective-permute-start.2 = (f32[1,16,7168]{2,1,0:T(8,128)}, f32[1,16,7168]{2,1,0:T(8,128)}, u32[]{:S(2)}, u32[]{:S(2)}) collective-permute-start(f32[1,16,7168]{2,1,0:T(8,128)} %collective-permute-done), channel_id=1, source_target_pairs={{0,30},{2,0},{4,2},{6,4},{8,6},{10,8},{12,10},{14,12},{16,14},{18,... | collective-permute-start | bytes 1376264 | tf_op jit(solution)/shard_map/ppermute | solution.py:19
  223.1 6.3 %collective-permute-done.3 = f32[1,16,7168]{2,1,0:T(8,128)} collective-permute-done((f32[1,16,7168]{2,1,0:T(8,128)S(1)}, f32[1,16,7168]{2,1,0:T(8,128)}, u32[]{:S(2)}, u32[]{:S(2)}) %collective-permute-start.3) | collective-permute-done | bytes 458784 | tf_op jit(solution)/shard_map/ppermute | solution.py:17
  230.4 3.7 %collective-permute-start.4 = (f32[1,16,7168]{2,1,0:T(8,128)}, f32[1,16,7168]{2,1,0:T(8,128)}, u32[]{:S(2)}, u32[]{:S(2)}) collective-permute-start(f32[1,16,7168]{2,1,0:T(8,128)} %collective-permute-done.2), channel_id=1, source_target_pairs={{0,30},{2,0},{4,2},{6,4},{8,6},{10,8},{12,10},{14,12},{16,14},{18,... | collective-permute-start | bytes 1376264 | tf_op jit(solution)/shard_map/ppermute | solution.py:19
  234.1 6.3 %collective-permute-done.5 = f32[1,16,7168]{2,1,0:T(8,128)} collective-permute-done((f32[1,16,7168]{2,1,0:T(8,128)}, f32[1,16,7168]{2,1,0:T(8,128)}, u32[]{:S(2)}, u32[]{:S(2)}) %collective-permute-start.5) | collective-permute-done | bytes 458784 | tf_op jit(solution)/shard_map/ppermute | solution.py:17
  240.3 2.3 collective-permute-start.7
  245.7 5.6 %collective-permute-done.7 = f32[1,16,7168]{2,1,0:T(8,128)} collective-permute-done((f32[1,16,7168]{2,1,0:T(8,128)}, f32[1,16,7168]{2,1,0:T(8,128)}, u32[]{:S(2)}, u32[]{:S(2)}) %collective-permute-start.7) | collective-permute-done | bytes 458784 | tf_op jit(solution)/shard_map/ppermute | solution.py:17
  251.4 4.5 %collective-permute-start.9 = (f32[1,16,7168]{2,1,0:T(8,128)}, f32[1,16,7168]{2,1,0:T(8,128)}, u32[]{:S(2)}, u32[]{:S(2)}) collective-permute-start(f32[1,16,7168]{2,1,0:T(8,128)} %collective-permute-done.7), channel_id=1, source_target_pairs={{0,2},{2,4},{4,6},{6,8},{8,10},{10,12},{12,14},{14,16},{16,18},{18... | collective-permute-start | bytes 1376264 | tf_op jit(solution)/shard_map/ppermute | solution.py:17
  256.5 5.9 %collective-permute-done.9 = f32[1,16,7168]{2,1,0:T(8,128)} collective-permute-done((f32[1,16,7168]{2,1,0:T(8,128)}, f32[1,16,7168]{2,1,0:T(8,128)}, u32[]{:S(2)}, u32[]{:S(2)}) %collective-permute-start.9) | collective-permute-done | bytes 458784 | tf_op jit(solution)/shard_map/ppermute | solution.py:17
  262.4 6.7 %collective-permute-start.11 = (f32[1,16,7168]{2,1,0:T(8,128)}, f32[1,16,7168]{2,1,0:T(8,128)}, u32[]{:S(2)}, u32[]{:S(2)}) collective-permute-start(f32[1,16,7168]{2,1,0:T(8,128)} %collective-permute-done.9), channel_id=1, source_target_pairs={{0,2},{2,4},{4,6},{6,8},{8,10},{10,12},{12,14},{14,16},{16,18},{18... | collective-permute-start | bytes 1376264 | tf_op jit(solution)/shard_map/ppermute | solution.py:17
  272.0 3.0 collective-permute-done.11
  274.9 6.1 %collective-permute-start.13 = (f32[1,16,7168]{2,1,0:T(8,128)}, f32[1,16,7168]{2,1,0:T(8,128)}, u32[]{:S(2)}, u32[]{:S(2)}) collective-permute-start(f32[1,16,7168]{2,1,0:T(8,128)} %collective-permute-done.11), channel_id=1, source_target_pairs={{0,2},{2,4},{4,6},{6,8},{8,10},{10,12},{12,14},{14,16},{16,18},{18... | collective-permute-start | bytes 1376264 | tf_op jit(solution)/shard_map/ppermute | solution.py:17
  281.1 34.9 %all-reduce = f32[16]{0:T(128)S(1)} all-reduce(f32[16]{0:T(128)S(1)} %dynamic-update-slice), channel_id=1, replica_groups=mesh['seq'=16,'tp'=2] {'seq'}, use_global_device_ids=true, to_apply=%add | all-reduce | flops 16 | bytes 128
  317.9 5.5 %all-to-all-start.1 = ((bf16[2,64,2048]{2,1,0:T(8,128)(2,1)}), bf16[2,64,2048]{2,1,0:T(8,128)(2,1)S(1)}, u32[]{:S(2)}, u32[]{:S(2)}) async-start(bf16[2,64,2048]{2,1,0:T(8,128)(2,1)} %bitcast.10), calls=%async_computation.1 | async-start | bytes 1048576 | tf_op jit(solution)/shard_map/all_to_all | solution.py:79
  325.3 7.0 %all-to-all-done.1 = bf16[2,64,2048]{2,1,0:T(8,128)(2,1)S(1)} async-done(((bf16[2,64,2048]{2,1,0:T(8,128)(2,1)}), bf16[2,64,2048]{2,1,0:T(8,128)(2,1)S(1)}, u32[]{:S(2)}, u32[]{:S(2)}) %all-to-all-start.1) | async-done | bytes 524320 | tf_op jit(solution)/shard_map/all_to_all | solution.py:79
  333.2 6.3 %multiply_add_fusion = f32[4,16,7168]{2,1,0:T(8,128)} fusion(f32[16,7168]{1,0:T(8,128)} %bitcast.48, f32[4]{0:T(128)S(1)} %get-tuple-element.37, f32[16,7168]{1,0:T(8,128)} %bitcast.46, f32[4]{0:T(128)S(1)} %get-tuple-element.23, f32[16,7168]{1,0:T(8,128)} %bitcast.44, f32[4]{0:T(128)S(1)} %get-tuple-element.24, f32[16,7168]{1,0:T(8,128)} %bitcast.42, ...), kind=kLoop, calls=%fused_computation.10 | loop fusion | flops 14221312 | bytes 9175296 | tf_op jit(solution)/shard_map/add | solution.py:21
  339.5 3.5 %fusion.5 = f32[4,16,2048]{2,0,1:T(4,128)S(1)} fusion(f32[16,16,2048]{2,1,0:T(8,128)} %bitcast.103, f32[4]{0:T(128)S(1)} %add_convert_fusion, f32[16]{0:T(128)S(1)} %all-reduce), kind=kOutput, calls=%fused_computation.8 | convolution fusion | flops 25165888 | bytes 2621520 | tf_op jit(solution)/shard_map/ns,nrd->srd/dot_general | solution.py:100
  (64 shorter events, 19.4 us)
Async XLA Ops:
  7.2 191.2 %copy-start = (bf16[128,7168]{1,0:T(8,128)(2,1)S(1)}, bf16[128,7168]{1,0:T(8,128)(2,1)}, u32[]{:S(2)}) copy-start(bf16[128,7168]{1,0:T(8,128)(2,1)} %param.8) | copy-start | bytes 5505028
  7.2 56.1 %all-gather.5.cloned.1.call-start = ((), (), s32[]{:S(2)}) async-start(), calls=%async_computation.2 | async-start | bytes 4456448 | tf_op jit(solution)/shard_map/all_gather | solution.py:43
  7.9 169.6 %all-gather.7.cloned.1.call-start = ((), (), s32[]{:S(2)}) async-start(), calls=%async_computation.3 | async-start | bytes 15597568 | tf_op jit(solution)/shard_map/all_gather | solution.py:44
  10.5 59.4 %all-to-all-start = ((bf16[64,2,2048]{2,0,1:T(8,128)(2,1)}), bf16[64,2,2048]{2,0,1:T(8,128)(2,1)S(1)}, u32[]{:S(2)}, u32[]{:S(2)}) async-start(bf16[64,2,2048]{2,0,1:T(8,128)(2,1)} %bitcast.95), calls=%async_computation | async-start | bytes 1048576 | tf_op jit(solution)/shard_map/all_to_all | solution.py:62
  14.8 324.7 %all-gather.9.cloned.1.call-start = ((), (), s32[]{:S(2)}) async-start(), calls=%async_computation.4 | async-start | bytes 2228224 | tf_op jit(solution)/shard_map/all_gather | solution.py:97
  199.0 70.2 %copy-start.4 = (u32[32]{0:T(128)S(1)}, u32[32]{0:T(128)}, u32[]{:S(2)}) copy-start(u32[32]{0:T(128)} %constant.119) | copy-start | bytes 388
  199.0 70.7 %copy-start.3 = (s32[64]{0:T(128)S(1)}, s32[64]{0:T(128)}, u32[]{:S(2)}) copy-start(s32[64]{0:T(128)} %param.13) | copy-start | bytes 772
  207.8 10.7 %collective-permute-start.1 = (f32[1,16,7168]{2,1,0:T(8,128)S(1)}, f32[1,16,7168]{2,1,0:T(8,128)S(1)}, u32[]{:S(2)}, u32[]{:S(2)}) collective-permute-start(f32[1,16,7168]{2,1,0:T(8,128)S(1)} %bitcast.105), channel_id=1, source_target_pairs={{0,2},{2,4},{4,6},{6,8},{8,10},{10,12},{12,14},{14,16},{16,18},{18... | collective-permute-start | bytes 1376264 | tf_op jit(solution)/shard_map/ppermute | solution.py:17
  207.8 11.0 %collective-permute-start = (f32[1,16,7168]{2,1,0:T(8,128)S(1)}, f32[1,16,7168]{2,1,0:T(8,128)}, u32[]{:S(2)}, u32[]{:S(2)}) collective-permute-start(f32[1,16,7168]{2,1,0:T(8,128)S(1)} %bitcast.106), channel_id=1, source_target_pairs={{0,30},{2,0},{4,2},{6,4},{8,6},{10,8},{12,10},{14,12},{16,14},{18,... | collective-permute-start | bytes 1376264 | tf_op jit(solution)/shard_map/ppermute | solution.py:19
  218.5 10.8 %collective-permute-start.3 = (f32[1,16,7168]{2,1,0:T(8,128)S(1)}, f32[1,16,7168]{2,1,0:T(8,128)}, u32[]{:S(2)}, u32[]{:S(2)}) collective-permute-start(f32[1,16,7168]{2,1,0:T(8,128)S(1)} %collective-permute-done.1), channel_id=1, source_target_pairs={{0,2},{2,4},{4,6},{6,8},{8,10},{10,12},{12,14},{14,16},{16,18},{18... | collective-permute-start | bytes 1376264 | tf_op jit(solution)/shard_map/ppermute | solution.py:17
  219.3 11.0 %collective-permute-start.2 = (f32[1,16,7168]{2,1,0:T(8,128)}, f32[1,16,7168]{2,1,0:T(8,128)}, u32[]{:S(2)}, u32[]{:S(2)}) collective-permute-start(f32[1,16,7168]{2,1,0:T(8,128)} %collective-permute-done), channel_id=1, source_target_pairs={{0,30},{2,0},{4,2},{6,4},{8,6},{10,8},{12,10},{14,12},{16,14},{18,... | collective-permute-start | bytes 1376264 | tf_op jit(solution)/shard_map/ppermute | solution.py:19
  229.3 11.0 %collective-permute-start.5 = (f32[1,16,7168]{2,1,0:T(8,128)}, f32[1,16,7168]{2,1,0:T(8,128)}, u32[]{:S(2)}, u32[]{:S(2)}) collective-permute-start(f32[1,16,7168]{2,1,0:T(8,128)} %collective-permute-done.3), channel_id=1, source_target_pairs={{0,2},{2,4},{4,6},{6,8},{8,10},{10,12},{12,14},{14,16},{16,18},{18... | collective-permute-start | bytes 1376264 | tf_op jit(solution)/shard_map/ppermute | solution.py:17
  230.4 13.2 %collective-permute-start.4 = (f32[1,16,7168]{2,1,0:T(8,128)}, f32[1,16,7168]{2,1,0:T(8,128)}, u32[]{:S(2)}, u32[]{:S(2)}) collective-permute-start(f32[1,16,7168]{2,1,0:T(8,128)} %collective-permute-done.2), channel_id=1, source_target_pairs={{0,30},{2,0},{4,2},{6,4},{8,6},{10,8},{12,10},{14,12},{16,14},{18,... | collective-permute-start | bytes 1376264 | tf_op jit(solution)/shard_map/ppermute | solution.py:19
  240.3 11.0 %collective-permute-start.7 = (f32[1,16,7168]{2,1,0:T(8,128)}, f32[1,16,7168]{2,1,0:T(8,128)}, u32[]{:S(2)}, u32[]{:S(2)}) collective-permute-start(f32[1,16,7168]{2,1,0:T(8,128)} %collective-permute-done.5), channel_id=1, source_target_pairs={{0,2},{2,4},{4,6},{6,8},{8,10},{10,12},{12,14},{14,16},{16,18},{18... | collective-permute-start | bytes 1376264 | tf_op jit(solution)/shard_map/ppermute | solution.py:17
  243.6 12.2 %collective-permute-start.6 = (f32[1,16,7168]{2,1,0:T(8,128)}, f32[1,16,7168]{2,1,0:T(8,128)S(1)}, u32[]{:S(2)}, u32[]{:S(2)}) collective-permute-start(f32[1,16,7168]{2,1,0:T(8,128)} %collective-permute-done.4), channel_id=1, source_target_pairs={{0,30},{2,0},{4,2},{6,4},{8,6},{10,8},{12,10},{14,12},{16,14},{18,... | collective-permute-start | bytes 1376264 | tf_op jit(solution)/shard_map/ppermute | solution.py:19
  251.4 11.1 %collective-permute-start.9 = (f32[1,16,7168]{2,1,0:T(8,128)}, f32[1,16,7168]{2,1,0:T(8,128)}, u32[]{:S(2)}, u32[]{:S(2)}) collective-permute-start(f32[1,16,7168]{2,1,0:T(8,128)} %collective-permute-done.7), channel_id=1, source_target_pairs={{0,2},{2,4},{4,6},{6,8},{8,10},{10,12},{12,14},{14,16},{16,18},{18... | collective-permute-start | bytes 1376264 | tf_op jit(solution)/shard_map/ppermute | solution.py:17
  255.8 62.1 %copy-start.2 = (f32[1,16,7168]{2,1,0:T(8,128)}, f32[1,16,7168]{2,1,0:T(8,128)S(1)}, u32[]{:S(2)}) copy-start(f32[1,16,7168]{2,1,0:T(8,128)S(1)} %collective-permute-done.6) | copy-start | bytes 1376260
  255.8 15.9 %collective-permute-start.8 = (f32[1,16,7168]{2,1,0:T(8,128)S(1)}, f32[1,16,7168]{2,1,0:T(8,128)}, u32[]{:S(2)}, u32[]{:S(2)}) collective-permute-start(f32[1,16,7168]{2,1,0:T(8,128)S(1)} %collective-permute-done.6), channel_id=1, source_target_pairs={{0,30},{2,0},{4,2},{6,4},{8,6},{10,8},{12,10},{14,12},{16,14},{18,... | collective-permute-start | bytes 1376264 | tf_op jit(solution)/shard_map/ppermute | solution.py:19
  262.4 12.5 %collective-permute-start.11 = (f32[1,16,7168]{2,1,0:T(8,128)}, f32[1,16,7168]{2,1,0:T(8,128)}, u32[]{:S(2)}, u32[]{:S(2)}) collective-permute-start(f32[1,16,7168]{2,1,0:T(8,128)} %collective-permute-done.9), channel_id=1, source_target_pairs={{0,2},{2,4},{4,6},{6,8},{8,10},{10,12},{12,14},{14,16},{16,18},{18... | collective-permute-start | bytes 1376264 | tf_op jit(solution)/shard_map/ppermute | solution.py:17
  271.7 44.6 %collective-permute-start.10 = (f32[1,16,7168]{2,1,0:T(8,128)}, f32[1,16,7168]{2,1,0:T(8,128)}, u32[]{:S(2)}, u32[]{:S(2)}) collective-permute-start(f32[1,16,7168]{2,1,0:T(8,128)} %collective-permute-done.8), channel_id=1, source_target_pairs={{0,30},{2,0},{4,2},{6,4},{8,6},{10,8},{12,10},{14,12},{16,14},{18,... | collective-permute-start | bytes 1376264 | tf_op jit(solution)/shard_map/ppermute | solution.py:19
  274.9 41.4 %collective-permute-start.13 = (f32[1,16,7168]{2,1,0:T(8,128)}, f32[1,16,7168]{2,1,0:T(8,128)}, u32[]{:S(2)}, u32[]{:S(2)}) collective-permute-start(f32[1,16,7168]{2,1,0:T(8,128)} %collective-permute-done.11), channel_id=1, source_target_pairs={{0,2},{2,4},{4,6},{6,8},{8,10},{10,12},{12,14},{14,16},{16,18},{18... | collective-permute-start | bytes 1376264 | tf_op jit(solution)/shard_map/ppermute | solution.py:17
  316.3 16.8 %collective-permute-start.12 = (f32[1,16,7168]{2,1,0:T(8,128)}, f32[1,16,7168]{2,1,0:T(8,128)}, u32[]{:S(2)}, u32[]{:S(2)}) collective-permute-start(f32[1,16,7168]{2,1,0:T(8,128)} %collective-permute-done.10), channel_id=1, source_target_pairs={{0,30},{2,0},{4,2},{6,4},{8,6},{10,8},{12,10},{14,12},{16,14},{18,... | collective-permute-start | bytes 1376264 | tf_op jit(solution)/shard_map/ppermute | solution.py:19
  316.4 16.8 %collective-permute-start.14 = (f32[1,16,7168]{2,1,0:T(8,128)}, f32[1,16,7168]{2,1,0:T(8,128)}, u32[]{:S(2)}, u32[]{:S(2)}) collective-permute-start(f32[1,16,7168]{2,1,0:T(8,128)} %collective-permute-done.13), channel_id=1, source_target_pairs={{0,2},{2,4},{4,6},{6,8},{8,10},{10,12},{12,14},{14,16},{16,18},{18... | collective-permute-start | bytes 1376264 | tf_op jit(solution)/shard_map/ppermute | solution.py:17
  317.9 14.4 %all-to-all-start.1 = ((bf16[2,64,2048]{2,1,0:T(8,128)(2,1)}), bf16[2,64,2048]{2,1,0:T(8,128)(2,1)S(1)}, u32[]{:S(2)}, u32[]{:S(2)}) async-start(bf16[2,64,2048]{2,1,0:T(8,128)(2,1)} %bitcast.10), calls=%async_computation.1 | async-start | bytes 1048576 | tf_op jit(solution)/shard_map/all_to_all | solution.py:79
  (1 other events, 0.8 us)
Sparse Core Ops, SparseCore 0:
  10.1 53.0 all-gather.4
  65.6 111.8 all-gather.6
  243.7 54.2 all-gather.8
